TPU v7x, 32 devices: a whole 2x2x4 slice. The times are simulated.
32 devices in a mesh: groups: 2 (over y), expert: 8 (over z, x), tensor: 2 (over core).
Axes of the slice: x: 2, y: 2, z: 4, core: 2. Of those that a mesh axis runs over, the one named last changes fastest.
Arguments:
- conv_input: bfloat16 [32, 8192], P(('groups', 'expert'), 'tensor'), parts along dimension 0, may hold values from -6 to 6
- gate_input: bfloat16 [32, 8192], P(('groups', 'expert'), 'tensor'), parts along dimension 0, may hold values from -6 to 6
- step_input: bfloat16 [32, 8192], P(('groups', 'expert'), 'tensor'), parts along dimension 0, may hold values from -6 to 6
- b_proj: float32 [32, 16], P(('groups', 'expert')), parts along dimension 0, may hold values from -6 to 6
- c_proj: float32 [32, 16], P(('groups', 'expert')), parts along dimension 0, may hold values from -6 to 6
- slot_ids: int32 [32], P(('groups', 'expert')), parts along dimension 0, may hold values from 0 to 15, as said below
- state_pool: bfloat16 [32, 16, 8192], P(('groups', 'expert'), None, 'tensor'), parts along dimension 0, may hold values from -6 to 6
- conv_pool: bfloat16 [32, 3, 8192], P(('groups', 'expert'), None, 'tensor'), parts along dimension 0, may hold values from -6 to 6
- conv_weight: float32 [4, 8192], P(None, 'tensor'), may hold values from -4 to 4
- conv_bias: float32 [8192], P('tensor'), may hold values from -4 to 4
- step_bias: float32 [8192], P('tensor'), may hold values from -4 to 0
- a_log: float32 [16, 8192], P(None, 'tensor'), may hold values from -1 to 2.5
- d_skip: float32 [8192], P('tensor'), may hold values from 0.5 to 1.5
- out_weight: bfloat16 [8192, 4096], P('tensor', 'expert'), may hold values from -0.0625 to 0.0625
- residual: bfloat16 [32, 4096], P(('groups', 'expert')), parts along dimension 0, may hold values from -6 to 6
- norm_gain: float32 [4096], replicated, may hold values from 0.5 to 1.5
- expert_ids: int32 [32, 2], P(('groups', 'expert')), parts along dimension 0, may hold values from 0 to 2, all different within a row
- expert_probs: bfloat16 [32, 2], P(('groups', 'expert')), parts along dimension 0, may hold values from 0.19921875 to 1
- gate_weight: bfloat16 [36864, 4096], P(('expert', 'tensor')), may hold values from -0.09375 to 0.09375
- up_weight: bfloat16 [36864, 4096], P(('expert', 'tensor')), may hold values from -0.09375 to 0.09375
- down_weight: bfloat16 [36864, 4096], P(('expert', 'tensor')), may hold values from -0.0546875 to 0.0546875
Outputs:
- layer_out: bfloat16 [32, 4096], P(('groups', 'expert')), parts along dimension 0
- new_state: bfloat16 [32, 16, 8192], P(('groups', 'expert'), None, 'tensor'), parts along dimension 0
There are 2 independent parts, one for each index of `groups`. A program takes and returns all parts, laid end to end along the dimension named above; an argument that names none is the same for every part. Nothing has to cross between parts.
Inputs may be any that keep to these rules, and one draw needn't show every extreme that they name: `slot_ids`: the rows of one index of expert (rows d*2 to (d+1)*2 - 1) use distinct slots among d*2 to (d+1)*2 - 1. `expert_ids`: each row names two different experts.
All inputs are finite; a program needn't handle non-finite values.
Results may differ from a plain program's by a relative error of at most 0.0063.
Values may be sent and summed in bfloat16 or wider, within the bound.
A program may use at most 128 MiB of HBM per device.

v0:
```python
import jax
import jax.numpy as jnp
from jax import lax
from jax.sharding import PartitionSpec as P

EXPERTS = 3
FF = 12288


def mamba_step(
    states,
    history,
    conv_input,
    gate_input,
    step_input,
    b_proj,
    c_proj,
    conv_weight,
    conv_bias,
    step_bias,
    a_log,
    d_skip,
):
    inputs = conv_input.astype(jnp.float32)
    conv_sum = conv_weight[-1] * inputs + conv_bias
    for lag in range(history.shape[1]):
        conv_sum = conv_sum + conv_weight[lag] * history[:, lag]
    conv_out = jax.nn.silu(conv_sum)
    step_size = jax.nn.softplus(step_input.astype(jnp.float32) + step_bias)
    state_rates = -jnp.exp(a_log)
    decay_rate = jnp.exp(step_size[:, None, :] * state_rates[None])
    state_next = decay_rate * states + (step_size * conv_out)[:, None, :] * b_proj[:, :, None]
    output = jnp.sum(c_proj[:, :, None] * state_next, axis=1) + d_skip * conv_out
    gated_out = (output * jax.nn.silu(gate_input.astype(jnp.float32))).astype(jnp.bfloat16)
    return (state_next, gated_out)


def expert_terms(rows, coefs, first_unit, gate_weight, up_weight, down_weight):
    dims = (((1,), (1,)), ((), ()))
    gate_act = lax.dot_general(rows, gate_weight, dims, preferred_element_type=jnp.float32)
    up_act = lax.dot_general(rows, up_weight, dims, preferred_element_type=jnp.float32)
    hidden = (jax.nn.silu(gate_act) * up_act).astype(jnp.bfloat16)
    units = gate_weight.shape[0]
    lower_expert = first_unit // FF
    boundary = (lower_expert + 1) * FF - first_unit
    column = jnp.arange(units, dtype=jnp.int32)[None, :]
    zeros_bf = jnp.zeros_like(hidden)
    lower_hidden = jnp.where(column < boundary, hidden, zeros_bf)
    upper_hidden = jnp.where(column >= boundary, hidden, zeros_bf)
    expert_range = jnp.arange(EXPERTS, dtype=jnp.int32)[None, :]
    wide_coefs = coefs.astype(jnp.float32)
    lower_coef = jnp.sum(wide_coefs * (expert_range == lower_expert).astype(jnp.float32), axis=1)
    upper_coef = jnp.sum(
        wide_coefs * (expert_range == lower_expert + 1).astype(jnp.float32), axis=1
    )
    lower_out = jnp.dot(lower_hidden, down_weight, preferred_element_type=jnp.float32)
    upper_out = jnp.dot(upper_hidden, down_weight, preferred_element_type=jnp.float32)
    return lower_coef[:, None] * lower_out + upper_coef[:, None] * upper_out


def local(
    conv_input,
    gate_input,
    step_input,
    b_proj,
    c_proj,
    slot_ids,
    state_pool,
    conv_pool,
    conv_weight,
    conv_bias,
    step_bias,
    a_log,
    d_skip,
    out_weight,
    residual,
    norm_gain,
    expert_ids,
    expert_probs,
    gate_weight,
    up_weight,
    down_weight,
):
    pool_dev = state_pool.shape[0]
    local_slot = slot_ids - lax.axis_index("expert") * pool_dev
    select = (local_slot[:, None] == jnp.arange(pool_dev, dtype=jnp.int32)[None, :]).astype(
        jnp.bfloat16
    )
    states = jnp.einsum("rp,pnc->rnc", select, state_pool, preferred_element_type=jnp.float32)
    history = jnp.einsum("rp,pkc->rkc", select, conv_pool, preferred_element_type=jnp.float32)
    state_next, gated_out = mamba_step(
        states,
        history,
        conv_input,
        gate_input,
        step_input,
        b_proj,
        c_proj,
        conv_weight,
        conv_bias,
        step_bias,
        a_log,
        d_skip,
    )
    columns = jnp.dot(
        lax.all_gather(gated_out, "expert", axis=0, tiled=True),
        out_weight,
        preferred_element_type=jnp.float32,
    )
    returned_cols = lax.all_to_all(columns, "expert", split_axis=0, concat_axis=1, tiled=True)
    mixed = lax.psum(returned_cols, "tensor").astype(jnp.bfloat16)
    hidden_state = (residual.astype(jnp.float32) + mixed.astype(jnp.float32)).astype(jnp.bfloat16)
    wide = hidden_state.astype(jnp.float32)
    normed = (
        wide * lax.rsqrt(jnp.mean(wide * wide, axis=1, keepdims=True) + 1e-05) * norm_gain
    ).astype(jnp.bfloat16)
    probs = expert_probs.astype(jnp.float32)
    expert_range = jnp.arange(EXPERTS, dtype=jnp.int32)
    picked = (expert_ids[:, :, None] == expert_range[None, None, :]).astype(jnp.float32)
    coefs = jnp.sum(picked * probs[:, :, None], axis=1).astype(jnp.bfloat16)
    units = gate_weight.shape[0]
    first_unit = (
        lax.axis_index("expert") * lax.axis_size("tensor") + lax.axis_index("tensor")
    ) * units
    peers = lax.axis_size("expert")
    span = EXPERTS * FF // peers
    dest = jnp.arange(peers, dtype=jnp.int32)[:, None]
    intersection = (
        (expert_range[None, :] * FF < (dest + 1) * span)
        & ((expert_range[None, :] + 1) * FF > dest * span)
    ).astype(jnp.float32)
    chosen = jnp.sum(picked, axis=1)
    needed = jnp.dot(intersection, chosen.T, preferred_element_type=jnp.float32) > 0.5
    outgoing = jnp.where(needed[:, :, None], normed[None], jnp.zeros_like(normed)[None])
    out_coefs = jnp.broadcast_to(coefs[None], (peers, coefs.shape[0], coefs.shape[1]))
    rows_in = lax.all_to_all(outgoing, "expert", split_axis=0, concat_axis=0, tiled=True)
    coefs_in = lax.all_to_all(out_coefs, "expert", split_axis=0, concat_axis=0, tiled=True)
    flat_rows = rows_in.reshape(-1, rows_in.shape[2])
    flat_coefs = coefs_in.reshape(-1, coefs_in.shape[2])
    result = expert_terms(flat_rows, flat_coefs, first_unit, gate_weight, up_weight, down_weight)
    partial_value = result.reshape(rows_in.shape[0], rows_in.shape[1], rows_in.shape[2])
    returned = lax.all_to_all(partial_value, "expert", split_axis=0, concat_axis=0, tiled=True)
    routed = lax.psum(jnp.sum(returned, axis=0), "tensor")
    layer_out = (hidden_state.astype(jnp.float32) + routed).astype(jnp.bfloat16)
    return (layer_out, state_next.astype(jnp.bfloat16))


def solution(mesh):
    return jax.shard_map(
        local,
        mesh=mesh,
        in_specs=(
            P(("groups", "expert"), "tensor"),
            P(("groups", "expert"), "tensor"),
            P(("groups", "expert"), "tensor"),
            P(("groups", "expert"), None),
            P(("groups", "expert"), None),
            P(("groups", "expert")),
            P(("groups", "expert"), None, "tensor"),
            P(("groups", "expert"), None, "tensor"),
            P(None, "tensor"),
            P("tensor"),
            P("tensor"),
            P(None, "tensor"),
            P("tensor"),
            P("tensor", "expert"),
            P(("groups", "expert"), None),
            P(),
            P(("groups", "expert"), None),
            P(("groups", "expert"), None),
            P(("expert", "tensor"), None),
            P(("expert", "tensor"), None),
            P(("expert", "tensor"), None),
        ),
        out_specs=(P(("groups", "expert"), None), P(("groups", "expert"), None, "tensor")),
        check_vma=False,
    )
```

profile of v0, /device:TPU:0, one launch (start us, length us, event | category | flops | bytes accessed | tf_op | source)
XLA Modules:
  0.0 134.9 jit_solution(396333789273066836)
XLA Ops:
  0.7 0.8 copy.73
  1.4 0.8 copy.71
  2.2 1.1 fusion.39
  3.3 1.0 exponential_negate_fusion
  4.3 0.7 broadcast_subtract_fusion
  4.9 1.0 fusion.32
  6.0 0.9 fusion.37
  6.9 1.1 fusion.38
  8.0 0.8 fusion.24
  8.8 32.3 %all-gather = bf16[8,2,4096]{2,1,0:T(2,128)(2,1)S(1)} all-gather(bf16[1,2,4096]{2,1,0:T(2,128)(2,1)S(1)} %fusion.24), channel_id=1, replica_groups=mesh['groups'=2,'expert'=8,'tensor'=2] {'expert'}, dimensions={0}, use_global_device_ids=true | all-gather | bytes 147456 | tf_op jit(solution)/shard_map/all_gather | solution.py:106
  41.2 2.8 %fusion.40 = f32[16,512]{1,0:T(8,128)S(1)} fusion(bf16[16,4096]{1,0:T(8,128)(2,1)S(1)} %reshape.106, bf16[4096,512]{1,0:T(8,128)(2,1)} %param.34), kind=kOutput, calls=%fused_computation.76 | convolution fusion | flops 67108864 | bytes 4358144 | tf_op jit(solution)/shard_map/dot_general | solution.py:105
  44.0 0.7 all_to_all.23
  44.7 5.5 %all-to-all-start = ((f32[8,2,512]{2,1,0:T(2,128)}), f32[8,2,512]{2,1,0:T(2,128)S(1)}, u32[]{:S(2)}, u32[]{:S(2)}) async-start(f32[8,2,512]{2,1,0:T(2,128)} %all_to_all.23), calls=%async_computation | async-start | bytes 65536 | tf_op jit(solution)/shard_map/all_to_all | solution.py:110
  50.2 0.7 convert_element_type.85
  50.8 0.8 convert_reduce_fusion
  51.9 5.0 %all-to-all-done = f32[8,2,512]{2,1,0:T(2,128)S(1)} async-done(((f32[8,2,512]{2,1,0:T(2,128)}), f32[8,2,512]{2,1,0:T(2,128)S(1)}, u32[]{:S(2)}, u32[]{:S(2)}) %all-to-all-start) | async-done | bytes 32800 | tf_op jit(solution)/shard_map/all_to_all | solution.py:110
  57.4 3.3 %all-to-all-start.1 = ((bf16[8,2,3]{2,1,0:T(2,128)(2,1)}), bf16[8,2,3]{2,1,0:T(2,128)(2,1)S(1)}, u32[]{:S(2)}, u32[]{:S(2)}) async-start(bf16[8,2,3]{2,1,0:T(2,128)(2,1)} %broadcast_in_dim.29), calls=%async_computation.1 | async-start | bytes 8192 | tf_op jit(solution)/shard_map/all_to_all | solution.py:137
  60.8 3.4 %psum.14 = bf16[2,4096]{1,0:T(2,128)(2,1)S(1)} all-reduce(f32[2,4096]{1,0:T(2,128)S(1)} %bitcast.56), channel_id=1, replica_groups=mesh['groups'=2,'expert'=8,'tensor'=2] {'tensor'}, use_global_device_ids=true, to_apply=%region_1.2 | all-reduce | flops 8192 | bytes 49152 | tf_op jit(solution)/shard_map/psum | solution.py:111
  64.2 0.9 fusion.13
  65.0 0.8 fusion.15
  65.9 0.8 broadcast_select_fusion
  67.1 5.5 %all-to-all-start.2 = ((bf16[8,2,4096]{2,1,0:T(2,128)(2,1)}), bf16[8,2,4096]{2,1,0:T(2,128)(2,1)S(1)}, u32[]{:S(2)}, u32[]{:S(2)}) async-start(bf16[8,2,4096]{2,1,0:T(2,128)(2,1)} %broadcast_select_fusion), calls=%async_computation.2 | async-start | bytes 262144 | tf_op jit(solution)/shard_map/all_to_all | solution.py:136
  73.1 6.9 %all-to-all-done.2 = bf16[8,2,4096]{2,1,0:T(2,128)(2,1)S(1)} async-done(((bf16[8,2,4096]{2,1,0:T(2,128)(2,1)}), bf16[8,2,4096]{2,1,0:T(2,128)(2,1)S(1)}, u32[]{:S(2)}, u32[]{:S(2)}) %all-to-all-start.2) | async-done | bytes 131104 | tf_op jit(solution)/shard_map/all_to_all | solution.py:136
  80.1 11.3 %fusion.41 = f32[16,2304]{1,0:T(8,128)S(1)} fusion(bf16[16,4096]{1,0:T(8,128)(2,1)S(1)} %reshape.103, bf16[2304,4096]{1,0:T(8,128)(2,1)} %param.39), kind=kOutput, calls=%fused_computation.77 | convolution fusion | flops 301989888 | bytes 19152896 | tf_op jit(solution)/shard_map/dot_general | solution.py:40
  91.5 11.3 %fusion.2 = bf16[16,2304]{1,0:T(8,128)(2,1)S(1)} fusion(bf16[16,4096]{1,0:T(8,128)(2,1)S(1)} %reshape.103, bf16[2304,4096]{1,0:T(8,128)(2,1)} %param.40, f32[16,2304]{1,0:T(8,128)S(1)} %fusion.41), kind=kOutput, calls=%fused_computation.6 | convolution fusion | flops 302211072 | bytes 19226624 | tf_op jit(solution)/shard_map/dot_general | solution.py:41
  102.8 7.7 %convolution_multiply_fusion.2 = f32[16,4096]{1,0:T(8,128)S(1)} fusion(bf16[2304,4096]{1,0:T(8,128)(2,1)} %param.41, f32[16]{0:T(128)S(1)} %mul.245, bf16[16,2304]{1,0:T(8,128)(2,1)S(1)} %fusion.2, pred[2304]{0:T(1024)(128)(4,1)S(1)} %get-tuple-element.38), kind=kOutput, calls=%fused_computation.4 | convolution fusion | flops 302092288 | bytes 19212608 | tf_op jit(solution)/shard_map/dot_general | solution.py:56
  110.5 7.7 %fusion.1 = f32[16,4096]{1,0:T(8,128)S(1)} fusion(f32[16,4096]{1,0:T(8,128)S(1)} %convolution_multiply_fusion.2, bf16[2304,4096]{1,0:T(8,128)(2,1)} %param.41, f32[16]{0:T(128)S(1)} %mul.262, bf16[16,2304]{1,0:T(8,128)(2,1)S(1)} %fusion.2, pred[2304]{0:T(1024)(128)(4,1)S(1)} %get-tuple-element.37), kind=kOutput, calls=%fused_computation.3 | convolution fusion | flops 302157824 | bytes 19474752 | tf_op jit(solution)/shard_map/dot_general | solution.py:57
  118.2 0.8 reshape.104
  119.1 3.4 %all-to-all-start.3 = ((f32[8,2,4096]{2,1,0:T(2,128)}), f32[8,2,4096]{2,1,0:T(2,128)S(1)}, u32[]{:S(2)}, u32[]{:S(2)}) async-start(f32[8,2,4096]{2,1,0:T(2,128)} %reshape.104), calls=%async_computation.3 | async-start | bytes 524288 | tf_op jit(solution)/shard_map/all_to_all | solution.py:142
  122.5 0.9 copy.79
  123.4 7.4 %all-to-all-done.3 = f32[8,2,4096]{2,1,0:T(2,128)S(1)} async-done(((f32[8,2,4096]{2,1,0:T(2,128)}), f32[8,2,4096]{2,1,0:T(2,128)S(1)}, u32[]{:S(2)}, u32[]{:S(2)}) %all-to-all-start.3) | async-done | bytes 262176 | tf_op jit(solution)/shard_map/all_to_all | solution.py:142
  130.9 3.4 %psum.15 = f32[2,4096]{1,0:T(2,128)S(1)} all-reduce(f32[2,4096]{1,0:T(2,128)S(1)} %reduce_sum.69), channel_id=1, replica_groups=mesh['groups'=2,'expert'=8,'tensor'=2] {'tensor'}, use_global_device_ids=true, to_apply=%region_8.9 | all-reduce | flops 8192 | bytes 65536 | tf_op jit(solution)/shard_map/psum | solution.py:143
  (21 shorter events, 2.7 us)
Async XLA Ops:
  0.6 6.3 %copy-start = (bf16[2,16,4096]{2,1,0:T(8,128)(2,1)S(1)}, bf16[2,16,4096]{2,1,0:T(8,128)(2,1)}, u32[]{:S(2)}) copy-start(bf16[2,16,4096]{2,1,0:T(8,128)(2,1)} %param.27) | copy-start | bytes 786436
  44.7 12.1 %all-to-all-start = ((f32[8,2,512]{2,1,0:T(2,128)}), f32[8,2,512]{2,1,0:T(2,128)S(1)}, u32[]{:S(2)}, u32[]{:S(2)}) async-start(f32[8,2,512]{2,1,0:T(2,128)} %all_to_all.23), calls=%async_computation | async-start | bytes 65536 | tf_op jit(solution)/shard_map/all_to_all | solution.py:110
  57.4 9.7 %all-to-all-start.1 = ((bf16[8,2,3]{2,1,0:T(2,128)(2,1)}), bf16[8,2,3]{2,1,0:T(2,128)(2,1)S(1)}, u32[]{:S(2)}, u32[]{:S(2)}) async-start(bf16[8,2,3]{2,1,0:T(2,128)(2,1)} %broadcast_in_dim.29), calls=%async_computation.1 | async-start | bytes 8192 | tf_op jit(solution)/shard_map/all_to_all | solution.py:137
  67.1 13.0 %all-to-all-start.2 = ((bf16[8,2,4096]{2,1,0:T(2,128)(2,1)}), bf16[8,2,4096]{2,1,0:T(2,128)(2,1)S(1)}, u32[]{:S(2)}, u32[]{:S(2)}) async-start(bf16[8,2,4096]{2,1,0:T(2,128)(2,1)} %broadcast_select_fusion), calls=%async_computation.2 | async-start | bytes 262144 | tf_op jit(solution)/shard_map/all_to_all | solution.py:136
  119.1 11.7 %all-to-all-start.3 = ((f32[8,2,4096]{2,1,0:T(2,128)}), f32[8,2,4096]{2,1,0:T(2,128)S(1)}, u32[]{:S(2)}, u32[]{:S(2)}) async-start(f32[8,2,4096]{2,1,0:T(2,128)} %reshape.104), calls=%async_computation.3 | async-start | bytes 524288 | tf_op jit(solution)/shard_map/all_to_all | solution.py:142
where the time goes:
time: 136 us; the launch traced here: 135 us
  matrix products  43.3 us (32%)
  blocking collectives  39.2 us (29%)
  waiting for transfers between devices  19.8 us (15%)
  starting transfers between devices  17.7 us (13%)
  other arithmetic  8.12 us (6%)
  local copies, waits for them, and re-layouts  6.19 us (5%)
    all_gather x1, blocking collectives, local(): lax.all_gather(gated_out, 'expert', axis=0, tiled=True)  32.3 us
    dot_general x1, matrix products, expert_terms(): lax.dot_general(rows, up_weight, dims, preferred_element_type=jnp.float32)  11.3 us
    dot_general x1, matrix products, expert_terms(): lax.dot_general(rows, gate_weight, dims, preferred_element_type=jnp.float32)  11.3 us
    dot_general x1, matrix products, expert_terms(): jnp.dot(lower_hidden, down_weight, preferred_element_type=jnp.float32)  7.7 us
    dot_general x1, matrix products, expert_terms(): jnp.dot(upper_hidden, down_weight, preferred_element_type=jnp.float32)  7.7 us
    all_to_all x1, waiting for transfers between devices, local(): lax.all_to_all(partial_value, 'expert', split_axis=0, concat_axis=0, tile...  7.44 us
    all_to_all x1, waiting for transfers between devices, local(): lax.all_to_all(outgoing, 'expert', split_axis=0, concat_axis=0, tiled=True)  6.94 us
    all_to_all x1, starting transfers between devices, local(): lax.all_to_all(outgoing, 'expert', split_axis=0, concat_axis=0, tiled=True)  5.49 us
  transfers between devices with their start and end apart: 4, of which 4 were waited for; matrix products, arithmetic and copies ran while one was open for 4% of the time, Pallas kernels for 0%

commit v1 on v0

v1 whole, which is shorter than its diff:
```python
import functools

import jax
import jax.numpy as jnp
from jax import lax
from jax.experimental import pallas as pl
from jax.experimental.pallas import tpu as pltpu
from jax.sharding import PartitionSpec as P

EXPERTS = 3
LANES = 128
F32 = jnp.float32
BF16 = jnp.bfloat16
TRANS = (((1,), (1,)), ((), ()))
MESH = pl.DeviceIdType.MESH
NJ = 4
SMALL = 16


def unit_block(units):
    for block in (256, 384, 128):
        if units % block == 0:
            return block
    return units


def kernel(
    peers,
    slots,
    *refs,
):
    small_hbm = refs[:SMALL]
    outw_hbm, gate_hbm, up_hbm, down_hbm = refs[SMALL : SMALL + 4]
    out_ref, ns_hbm = refs[SMALL + 4 : SMALL + 6]
    small = refs[SMALL + 6 : 2 * SMALL + 6]
    (
        small_sem,
        outw,
        outw_sem,
        gbuf,
        ubuf,
        dbuf,
        w_sem,
        gsend,
        grecv,
        gs_sem,
        gr_sem,
        rrecv,
        rs_sem,
        rr_sem,
        gat,
        part,
        part_in,
        part_sem,
        mix,
        mrecv,
        ms_sem,
        mr_sem,
        hid,
        normed,
        h3,
        osend,
        orecv,
        os_sem,
        or_sem,
        fin,
        fin_sem,
        nsbuf,
        ns_sem,
    ) = refs[2 * SMALL + 6 :]
    (
        conv_in,
        gate_in,
        step_in,
        b_proj,
        c_proj,
        pool,
        cpool,
        conv_w,
        conv_b,
        step_b,
        a_log,
        d_skip,
        resid,
        gain,
        ids,
        probs,
    ) = small
    e = lax.axis_index("expert")
    t = lax.axis_index("tensor")
    other = 1 - t
    nch, ub, d = gbuf.shape
    rows_dev, chl = conv_in.shape
    rows = rows_dev * peers
    units = nch * ub
    ff = units * peers * 2 // EXPERTS
    cb = outw.shape[1]
    half = d // 2
    nj2 = NJ // 2
    cw = d // NJ

    def peer(k):
        return lax.rem(e + k, peers)

    def each_peer(body):
        def step(k, carry):
            body(peer(k))
            return carry

        lax.fori_loop(1, peers, step, 0)

    barrier = pltpu.get_barrier_semaphore()
    pl.semaphore_signal(
        barrier, inc=1, device_id={"expert": e, "tensor": other}, device_id_type=MESH
    )

    def greet(p):
        pl.semaphore_signal(barrier, inc=1, device_id={"expert": p, "tensor": t}, device_id_type=MESH)
        pl.semaphore_signal(
            barrier, inc=1, device_id={"expert": p, "tensor": other}, device_id_type=MESH
        )

    each_peer(greet)

    loads = [
        pltpu.make_async_copy(src, dst, small_sem.at[i])
        for i, (src, dst) in enumerate(zip(small_hbm, small))
    ]
    for load in loads:
        load.start()
    outw_load = pltpu.make_async_copy(outw_hbm, outw, outw_sem)
    outw_load.start()

    def weight(which, c):
        src, dst = ((gate_hbm, gbuf), (up_hbm, ubuf), (down_hbm, dbuf))[which]
        return pltpu.make_async_copy(
            src.at[pl.ds(pl.multiple_of(c * ub, ub), ub)], dst.at[c], w_sem.at[which, c]
        )

    def start_gate_up(c, carry):
        weight(0, c).start()
        weight(1, c).start()
        return carry

    def start_down(c, carry):
        weight(2, c).start()
        return carry

    lax.fori_loop(0, nch, start_gate_up, 0)
    lax.fori_loop(0, nch, start_down, 0)
    for load in loads:
        load.wait()

    npool, ns = pool.shape[:2]
    eye = lax.broadcasted_iota(jnp.int32, (ns, ns), 0) == lax.broadcasted_iota(
        jnp.int32, (ns, ns), 1
    )

    def column(ref, r):
        return jnp.sum(
            jnp.where(eye, jnp.broadcast_to(ref[r : r + 1, :], (ns, ns)), 0.0),
            axis=1,
            keepdims=True,
        )

    b_cols = [column(b_proj, r) for r in range(rows_dev)]
    c_cols = [column(c_proj, r) for r in range(rows_dev)]
    local = [slots[r] - e * npool for r in range(rows_dev)]
    block = 512 if chl % 512 == 0 else chl
    taps = conv_w.shape[0]

    def mixer(i, carry):
        cols = pl.ds(pl.multiple_of(i * block, block), block)
        rates = jnp.exp(a_log[:, cols])
        xin = conv_in[:, cols].astype(F32)
        step_all = step_in[:, cols].astype(F32) + step_b[:, cols]
        step_all = jnp.maximum(step_all, 0.0) + jnp.log1p(jnp.exp(-jnp.abs(step_all)))
        gate_all = jax.nn.silu(gate_in[:, cols].astype(F32))
        weights = conv_w[:, cols]
        bias = conv_b[:, cols]
        skip = d_skip[:, cols]
        outs = []
        for r in range(rows_dev):
            hist = cpool[0, :, cols].astype(F32)
            state = pool[0, :, cols].astype(F32)
            for q in range(1, npool):
                mine = local[r] == q
                hist = jnp.where(mine, cpool[q, :, cols].astype(F32), hist)
                state = jnp.where(mine, pool[q, :, cols].astype(F32), state)
            acc = weights[taps - 1 : taps] * xin[r : r + 1] + bias
            for lag in range(taps - 1):
                acc = acc + weights[lag : lag + 1] * hist[lag : lag + 1]
            conv = jax.nn.silu(acc)
            size = step_all[r : r + 1]
            nxt = jnp.exp(-(size * rates)) * state + (size * conv) * b_cols[r]
            nsbuf[r, :, cols] = nxt.astype(BF16)
            outs.append(jnp.sum(c_cols[r] * nxt, axis=0, keepdims=True) + skip * conv)
        gated = jnp.concatenate(outs, axis=0) * gate_all
        gsend[:, cols] = gated.astype(BF16)
        return carry

    lax.fori_loop(0, chl // block, mixer, 0)
    lane = lax.broadcasted_iota(jnp.int32, (rows_dev, LANES), 1)
    wide_probs = probs[...].astype(F32)
    coefs = jnp.zeros((rows_dev, LANES), F32)
    for k in range(ids.shape[1]):
        coefs = coefs + jnp.where(lane == ids[:, k : k + 1], wide_probs[:, k : k + 1], 0.0)
    gsend[:, chl:] = coefs.astype(BF16)

    pl.semaphore_wait(barrier, 2 * peers - 1)

    def gated_copy(dst, slot, p):
        return pltpu.make_async_remote_copy(
            src_ref=gsend,
            dst_ref=grecv.at[dst],
            send_sem=gs_sem.at[slot],
            recv_sem=gr_sem.at[dst],
            device_id={"expert": p, "tensor": t},
            device_id_type=MESH,
        )

    def resid_copy(dst, slot, p):
        return pltpu.make_async_remote_copy(
            src_ref=resid,
            dst_ref=rrecv.at[dst],
            send_sem=rs_sem.at[slot],
            recv_sem=rr_sem.at[dst],
            device_id={"expert": p, "tensor": t},
            device_id_type=MESH,
        )

    def mix_copy(dst, slot, p):
        return pltpu.make_async_remote_copy(
            src_ref=mix,
            dst_ref=mrecv.at[dst],
            send_sem=ms_sem.at[slot],
            recv_sem=mr_sem.at[dst],
            device_id={"expert": p, "tensor": t},
            device_id_type=MESH,
        )

    each_peer(lambda p: gated_copy(e, p, p).start())
    each_peer(lambda p: resid_copy(e, p, p).start())
    ns_store = pltpu.make_async_copy(nsbuf, ns_hbm, ns_sem)
    ns_store.start()
    grecv[e] = gsend[...]
    rrecv[e] = resid[...]
    outw_load.wait()
    each_peer(lambda p: gated_copy(p, p, p).wait_recv())
    for p in range(peers):
        gat[p * rows_dev : (p + 1) * rows_dev, :] = grecv[p].astype(F32)

    part[...] = jnp.dot(gat[:, :chl].astype(BF16), outw[...], preferred_element_type=F32)
    swap = pltpu.make_async_remote_copy(
        src_ref=part,
        dst_ref=part_in,
        send_sem=part_sem.at[0],
        recv_sem=part_sem.at[1],
        device_id={"expert": e, "tensor": other},
        device_id_type=MESH,
    )
    swap.start()
    swap.wait_recv()
    mix[...] = (part[...] + part_in[...]).astype(BF16)
    each_peer(lambda p: mix_copy(e, p, p).start())
    mrecv[e] = mix[...]
    each_peer(lambda p: resid_copy(p, p, p).wait_recv())
    for p in range(peers):
        hid[p * rows_dev : (p + 1) * rows_dev, :] = rrecv[p].astype(F32)
    each_peer(lambda p: mix_copy(p, p, p).wait_recv())
    total = jnp.zeros((rows, 1), F32)
    for p in range(peers):
        cols = slice(p * cb, (p + 1) * cb)
        wide = (hid[:, cols] + mrecv[p].astype(F32)).astype(BF16).astype(F32)
        hid[:, cols] = wide
        total = total + jnp.sum(wide * wide, axis=1, keepdims=True)
    scale = lax.rsqrt(total / d + 1e-05)
    normed[...] = (hid[...] * scale * gain[...]).astype(BF16)

    first_unit = (e * 2 + t) * units
    lower = first_unit // ff
    boundary = (lower + 1) * ff - first_unit
    all_coefs = gat[:, chl:]
    wide_lane = lax.broadcasted_iota(jnp.int32, (rows, LANES), 1)
    lower_coef = jnp.sum(jnp.where(wide_lane == lower, all_coefs, 0.0), axis=1, keepdims=True)
    upper_coef = jnp.sum(jnp.where(wide_lane == lower + 1, all_coefs, 0.0), axis=1, keepdims=True)

    def gate_up(c, carry):
        weight(0, c).wait()
        weight(1, c).wait()
        x = normed[...]
        g = lax.dot_general(x, gbuf[c], TRANS, preferred_element_type=F32)
        u = lax.dot_general(x, ubuf[c], TRANS, preferred_element_type=F32)
        h = jax.nn.silu(g) * u
        unit = c * ub + lax.broadcasted_iota(jnp.int32, (rows, ub), 1)
        h3[c, :rows, :] = jnp.where(unit < boundary, h, 0.0).astype(BF16)
        h3[c, rows:, :] = jnp.where(unit >= boundary, h, 0.0).astype(BF16)
        return carry

    lax.fori_loop(0, nch, gate_up, 0)
    lax.fori_loop(0, nch, lambda c, carry: (weight(2, c).wait(), carry)[1], 0)

    def out_copy(j, slot, src, p):
        return pltpu.make_async_remote_copy(
            src_ref=osend.at[j, slot],
            dst_ref=orecv.at[j % nj2, src],
            send_sem=os_sem.at[j, slot],
            recv_sem=or_sem.at[j % nj2, src],
            device_id={"expert": p, "tensor": j // nj2},
            device_id_type=MESH,
        )

    me = e * 2 + t
    for j in range(NJ):
        cols = slice(j * cw, (j + 1) * cw)

        def down(c, acc):
            return acc + jnp.dot(h3[c], dbuf[c, :, cols], preferred_element_type=F32)

        acc = lax.fori_loop(0, nch, down, jnp.zeros((2 * rows, cw), F32))
        comb = (lower_coef * acc[:rows] + upper_coef * acc[rows:]).astype(BF16).astype(F32)
        for p in range(peers):
            osend[j, p] = comb[p * rows_dev : (p + 1) * rows_dev].astype(BF16)
        each_peer(lambda p: out_copy(j, p, me, p).start())

        @pl.when(t != j // nj2)
        def _():
            out_copy(j, e, me, e).start()

    mine = pl.ds(pl.multiple_of(t * half, half), half)
    own = hid[:rows_dev, mine]
    for p in range(1, peers):
        own = jnp.where(e == p, hid[p * rows_dev : (p + 1) * rows_dev, mine], own)
    for jj in range(nj2):
        orecv[jj, me] = osend[t * nj2 + jj, e]
    for jj in range(nj2):
        each_peer(lambda p: out_copy(jj, p, p * 2, p).wait_recv())
        each_peer(lambda p: out_copy(jj, p, p * 2 + 1, p).wait_recv())
        out_copy(jj, e, e * 2 + other, e).wait_recv()
        cols = slice(jj * cw, (jj + 1) * cw)
        routed = jnp.sum(orecv[jj].astype(F32), axis=0)
        fin[t, :, cols] = (own[:, cols] + routed).astype(BF16)
    done = pltpu.make_async_remote_copy(
        src_ref=fin.at[t],
        dst_ref=fin.at[t],
        send_sem=fin_sem.at[0],
        recv_sem=fin_sem.at[1],
        device_id={"expert": e, "tensor": other},
        device_id_type=MESH,
    )
    done.start()
    each_peer(lambda p: gated_copy(e, p, p).wait_send())
    each_peer(lambda p: resid_copy(e, p, p).wait_send())
    each_peer(lambda p: mix_copy(e, p, p).wait_send())
    swap.wait_send()
    for j in range(NJ):
        each_peer(lambda p: out_copy(j, p, me, p).wait_send())

        @pl.when(t != j // nj2)
        def _():
            out_copy(j, e, me, e).wait_send()

    ns_store.wait()
    done.wait()
    out_ref[:, :half] = fin[0]
    out_ref[:, half:] = fin[1]


def local(
    peers,
    conv_input,
    gate_input,
    step_input,
    b_proj,
    c_proj,
    slot_ids,
    state_pool,
    conv_pool,
    conv_weight,
    conv_bias,
    step_bias,
    a_log,
    d_skip,
    out_weight,
    residual,
    norm_gain,
    expert_ids,
    expert_probs,
    gate_weight,
    up_weight,
    down_weight,
):
    rows_dev, chl = conv_input.shape
    d = residual.shape[1]
    rows = rows_dev * peers
    units = gate_weight.shape[0]
    ub = unit_block(units)
    nch = units // ub
    cb = out_weight.shape[1]
    ns = state_pool.shape[1]
    cw = d // NJ
    small = (
        conv_input,
        gate_input,
        step_input,
        b_proj,
        c_proj,
        state_pool,
        conv_pool,
        conv_weight,
        conv_bias[None],
        step_bias[None],
        a_log,
        d_skip[None],
        residual,
        norm_gain[None],
        expert_ids,
        expert_probs,
    )
    sem = pltpu.SemaphoreType.DMA
    weights = pltpu.VMEM((nch, ub, d), BF16)
    hbm = pl.BlockSpec(memory_space=pl.ANY)
    return pl.pallas_call(
        functools.partial(kernel, peers),
        out_shape=(
            jax.ShapeDtypeStruct((rows_dev, d), BF16),
            jax.ShapeDtypeStruct((rows_dev, ns, chl), BF16),
        ),
        in_specs=[pl.BlockSpec(memory_space=pltpu.SMEM)] + [hbm] * (SMALL + 4),
        out_specs=(pl.BlockSpec(memory_space=pltpu.VMEM), hbm),
        scratch_shapes=[pltpu.VMEM(x.shape, x.dtype) for x in small]
        + [
            sem((SMALL,)),
            pltpu.VMEM((chl, cb), BF16),
            sem(()),
            weights,
            weights,
            weights,
            sem((3, nch)),
            pltpu.VMEM((rows_dev, chl + LANES), BF16),
            pltpu.VMEM((peers, rows_dev, chl + LANES), BF16),
            sem((peers,)),
            sem((peers,)),
            pltpu.VMEM((peers, rows_dev, d), BF16),
            sem((peers,)),
            sem((peers,)),
            pltpu.VMEM((rows, chl + LANES), F32),
            pltpu.VMEM((rows, cb), F32),
            pltpu.VMEM((rows, cb), F32),
            sem((2,)),
            pltpu.VMEM((rows, cb), BF16),
            pltpu.VMEM((peers, rows, cb), BF16),
            sem((peers,)),
            sem((peers,)),
            pltpu.VMEM((rows, d), F32),
            pltpu.VMEM((rows, d), BF16),
            pltpu.VMEM((nch, 2 * rows, ub), BF16),
            pltpu.VMEM((NJ, peers, rows_dev, cw), BF16),
            pltpu.VMEM((NJ // 2, 2 * peers, rows_dev, cw), BF16),
            sem((NJ, peers)),
            sem((NJ // 2, 2 * peers)),
            pltpu.VMEM((2, rows_dev, d // 2), BF16),
            sem((2,)),
            pltpu.VMEM((rows_dev, ns, chl), BF16),
            sem(()),
        ],
        compiler_params=pltpu.CompilerParams(
            collective_id=0, has_side_effects=True, vmem_limit_bytes=67043328
        ),
    )(slot_ids, *small, out_weight, gate_weight, up_weight, down_weight)


def solution(mesh):
    return jax.shard_map(
        functools.partial(local, mesh.shape["expert"]),
        mesh=mesh,
        in_specs=(
            P(("groups", "expert"), "tensor"),
            P(("groups", "expert"), "tensor"),
            P(("groups", "expert"), "tensor"),
            P(("groups", "expert"), None),
            P(("groups", "expert"), None),
            P(("groups", "expert")),
            P(("groups", "expert"), None, "tensor"),
            P(("groups", "expert"), None, "tensor"),
            P(None, "tensor"),
            P("tensor"),
            P("tensor"),
            P(None, "tensor"),
            P("tensor"),
            P("tensor", "expert"),
            P(("groups", "expert"), None),
            P(),
            P(("groups", "expert"), None),
            P(("groups", "expert"), None),
            P(("expert", "tensor"), None),
            P(("expert", "tensor"), None),
            P(("expert", "tensor"), None),
        ),
        out_specs=(P(("groups", "expert"), None), P(("groups", "expert"), None, "tensor")),
        check_vma=False,
    )
```

time: 136 us -> 49.8 us (0.37)
  Pallas kernels: 0 us -> 44.4 us
  matrix products: 43.3 us -> 0 us
  blocking collectives: 39.2 us -> 0 us
  waiting for transfers between devices: 19.8 us -> 0 us
  starting transfers between devices: 17.7 us -> 0 us
  other arithmetic: 8.12 us -> 0 us
  local copies, waits for them, and re-layouts: 6.19 us -> 4.48 us
    pallas_call x0 -> x1, Pallas kernels: none -> 44.4 us  [local(): pl.pallas_call(functools.partial(kernel, peers), out_shape=(jax.ShapeDtyp...]
    dot_general x8 -> x0, matrix products: 43.3 us -> none  [the longest x1 11.3 us: expert_terms(): lax.dot_general(rows, up_weight, dims, preferred_element_type=jnp.float32)]
    all_gather x1 -> x0, blocking collectives: 32.3 us -> none  [local(): lax.all_gather(gated_out, 'expert', axis=0, tiled=True)]
    all_to_all x4 -> x0, waiting for transfers between devices: 19.8 us -> none  [the longest x1 7.44 us: local(): lax.all_to_all(partial_value, 'expert', split_axis=0, concat_axis=0, tile...]
    all_to_all x4 -> x0, starting transfers between devices: 17.7 us -> none  [the longest x1 5.49 us: local(): lax.all_to_all(outgoing, 'expert', split_axis=0, concat_axis=0, tiled=True)]
    psum x2 -> x0, blocking collectives: 6.81 us -> none  [the longest x1 3.41 us: local(): mixed = lax.psum(returned_cols, 'tensor').astype(jnp.bfloat16)]
    convert_element_type x4 -> x0, other arithmetic: 2.1 us -> none  [the longest x1 0.81 us: local(): normed = (wide * lax.rsqrt(jnp.mean(wide * wide, axis=1, keepdims=True) +...]
    unnamed x6 -> x3, local copies, waits for them, and re-layouts: 2.47 us -> 4.48 us
  transfers between devices with their start and end apart: 4 -> 0, of which waited for: 4 -> 0; matrix products, arithmetic and copies ran while one was open for 4% -> 0% of each run, Pallas kernels for 0% -> 0%
where the time goes in v1:
time: 49.8 us; the launch traced here: 49.5 us
  Pallas kernels  44.4 us (89%)
  local copies, waits for them, and re-layouts  4.48 us (9%)
  between operations  0.64 us (1%)
    pallas_call x1, Pallas kernels, local(): pl.pallas_call(functools.partial(kernel, peers), out_shape=(jax.ShapeDtyp...  44.4 us
    unnamed x3, local copies, waits for them, and re-layouts  4.48 us

profile of v1, /device:TPU:0, one launch (start us, length us, event | category | flops | bytes accessed | tf_op | source)
XLA Modules:
  0.0 49.5 jit_solution(15026289934281220291)
XLA Ops:
  0.6 1.5 %copy.23.refs_6_ = bf16[2,3,4096]{2,1,0:T(4,128)(2,1)} copy(bf16[2,3,4096]{2,0,1:T(2,128)(2,1)} %param.28) | data formatting | bytes 98304 | tf_op args[7]
  2.1 44.4 %shard_map.212 = (bf16[2,4096]{1,0:T(2,128)(2,1)}, bf16[2,16,4096]{2,1,0:T(8,128)(2,1)}) custom-call(s32[2]{0:T(128)} %slots.1, bf16[2,4096]{1,0:T(2,128)(2,1)} %refs_0_.1, bf16[2,4096]{1,0:T(2,128)(2,1)} %refs_1_.1, bf16[2,4096]{1,0:T(2,128)(2,1)} %refs_2_.1, f32[2,16]{1,0:T(2,128)} %refs_3_.1, f32[2,16]{1,0:T(2,128)} %refs_4_.1, ...), custom_call_target="tpu_custom_call" | custom-call | tf_op jit(solution)/shard_map/pallas_call | solution.py:423
  46.5 1.3 %copy.26 = bf16[2,4096]{1,0:T(2,128)(2,1)} copy(bf16[2,4096]{1,0:T(2,128)(2,1)} %get-tuple-element.4) | data formatting | bytes 32768
  47.8 1.7 %copy.27 = bf16[2,16,4096]{2,1,0:T(8,128)(2,1)} copy(bf16[2,16,4096]{2,1,0:T(8,128)(2,1)} %get-tuple-element.5) | data formatting | bytes 524288

commit v2 on v1

--- a/solution.py
+++ b/solution.py
@@ -57,8 +57,9 @@
         ms_sem,
         mr_sem,
         hid,
-        normed,
-        h3,
+        gacc,
+        uacc,
+        h2,
         osend,
         orecv,
         os_sem,
@@ -132,10 +133,10 @@
     outw_load.start()
 
     def weight(which, c):
-        src, dst = ((gate_hbm, gbuf), (up_hbm, ubuf), (down_hbm, dbuf))[which]
-        return pltpu.make_async_copy(
-            src.at[pl.ds(pl.multiple_of(c * ub, ub), ub)], dst.at[c], w_sem.at[which, c]
-        )
+        src = (gate_hbm, up_hbm, down_hbm)[which]
+        span = pl.ds(pl.multiple_of(c * ub, ub), ub)
+        dst = (gbuf, ubuf)[which].at[c] if which < 2 else dbuf.at[span]
+        return pltpu.make_async_copy(src.at[span], dst, w_sem.at[which, c])
 
     def start_gate_up(c, carry):
         weight(0, c).start()
@@ -181,11 +182,11 @@
         skip = d_skip[:, cols]
         outs = []
         for r in range(rows_dev):
-            hist = cpool[0, :, cols].astype(F32)
+            hist = cpool[:, 0, cols].astype(F32)
             state = pool[0, :, cols].astype(F32)
             for q in range(1, npool):
                 mine = local[r] == q
-                hist = jnp.where(mine, cpool[q, :, cols].astype(F32), hist)
+                hist = jnp.where(mine, cpool[:, q, cols].astype(F32), hist)
                 state = jnp.where(mine, pool[q, :, cols].astype(F32), state)
             acc = weights[taps - 1 : taps] * xin[r : r + 1] + bias
             for lag in range(taps - 1):
@@ -267,15 +268,62 @@
     each_peer(lambda p: resid_copy(p, p, p).wait_recv())
     for p in range(peers):
         hid[p * rows_dev : (p + 1) * rows_dev, :] = rrecv[p].astype(F32)
-    each_peer(lambda p: mix_copy(p, p, p).wait_recv())
-    total = jnp.zeros((rows, 1), F32)
-    for p in range(peers):
-        cols = slice(p * cb, (p + 1) * cb)
+    def wait_gate_up(c, carry):
+        weight(0, c).wait()
+        weight(1, c).wait()
+        return carry
+
+    def products(x, cols, first):
+        for c in range(nch):
+            g = lax.dot_general(x, gbuf[c, :, cols], TRANS, preferred_element_type=F32)
+            u = lax.dot_general(x, ubuf[c, :, cols], TRANS, preferred_element_type=F32)
+            gacc[c] = g if first else gacc[c] + g
+            uacc[c] = u if first else uacc[c] + u
+
+    def arrived(p, cols):
         wide = (hid[:, cols] + mrecv[p].astype(F32)).astype(BF16).astype(F32)
         hid[:, cols] = wide
-        total = total + jnp.sum(wide * wide, axis=1, keepdims=True)
+        return wide
+
+    def squares(wide):
+        return jnp.sum(wide * wide, axis=1, keepdims=True)
+
+    lax.fori_loop(0, nch, wait_gate_up, 0)
+    if cb % LANES == 0 and peers % 2 == 0:
+
+        def nearest(k):
+            far = e // (peers // 2)
+            edge = e * (1 - far) + (peers - 1 - e) * far
+            inside = (2 * edge - k + 2 * peers) // (2 * peers)
+            step = (k + 1) // 2
+            odd = k % 2
+            paired = e + step * (2 * odd - 1)
+            single = k * (1 - far) + (peers - 1 - k) * far
+            return inside * paired + (1 - inside) * single
+
+        def columns_of(p):
+            return pl.ds(pl.multiple_of(p * cb, cb), cb)
+
+        cols = columns_of(e)
+        wide = arrived(e, cols)
+        products((wide * gain[:, cols]).astype(BF16), cols, True)
+
+        def next_block(k, total):
+            p = nearest(k)
+            mix_copy(p, p, p).wait_recv()
+            cols = columns_of(p)
+            wide = arrived(p, cols)
+            products((wide * gain[:, cols]).astype(BF16), cols, False)
+            return total + squares(wide)
+
+        total = lax.fori_loop(1, peers, next_block, squares(wide))
+    else:
+        each_peer(lambda p: mix_copy(p, p, p).wait_recv())
+        total = jnp.zeros((rows, 1), F32)
+        for p in range(peers):
+            total = total + squares(arrived(p, slice(p * cb, (p + 1) * cb)))
+        products((hid[...] * gain[...]).astype(BF16), slice(0, d), True)
     scale = lax.rsqrt(total / d + 1e-05)
-    normed[...] = (hid[...] * scale * gain[...]).astype(BF16)
 
     first_unit = (e * 2 + t) * units
     lower = first_unit // ff
@@ -285,19 +333,12 @@
     lower_coef = jnp.sum(jnp.where(wide_lane == lower, all_coefs, 0.0), axis=1, keepdims=True)
     upper_coef = jnp.sum(jnp.where(wide_lane == lower + 1, all_coefs, 0.0), axis=1, keepdims=True)
 
-    def gate_up(c, carry):
-        weight(0, c).wait()
-        weight(1, c).wait()
-        x = normed[...]
-        g = lax.dot_general(x, gbuf[c], TRANS, preferred_element_type=F32)
-        u = lax.dot_general(x, ubuf[c], TRANS, preferred_element_type=F32)
-        h = jax.nn.silu(g) * u
+    for c in range(nch):
+        h = jax.nn.silu(gacc[c] * scale) * (uacc[c] * scale)
         unit = c * ub + lax.broadcasted_iota(jnp.int32, (rows, ub), 1)
-        h3[c, :rows, :] = jnp.where(unit < boundary, h, 0.0).astype(BF16)
-        h3[c, rows:, :] = jnp.where(unit >= boundary, h, 0.0).astype(BF16)
-        return carry
-
-    lax.fori_loop(0, nch, gate_up, 0)
+        here = slice(c * ub, (c + 1) * ub)
+        h2[:rows, here] = jnp.where(unit < boundary, h, 0.0).astype(BF16)
+        h2[rows:, here] = jnp.where(unit >= boundary, h, 0.0).astype(BF16)
     lax.fori_loop(0, nch, lambda c, carry: (weight(2, c).wait(), carry)[1], 0)
 
     def out_copy(j, slot, src, p):
@@ -313,11 +354,7 @@
     me = e * 2 + t
     for j in range(NJ):
         cols = slice(j * cw, (j + 1) * cw)
-
-        def down(c, acc):
-            return acc + jnp.dot(h3[c], dbuf[c, :, cols], preferred_element_type=F32)
-
-        acc = lax.fori_loop(0, nch, down, jnp.zeros((2 * rows, cw), F32))
+        acc = jnp.dot(h2[...], dbuf[:, cols], preferred_element_type=F32)
         comb = (lower_coef * acc[:rows] + upper_coef * acc[rows:]).astype(BF16).astype(F32)
         for p in range(peers):
             osend[j, p] = comb[p * rows_dev : (p + 1) * rows_dev].astype(BF16)
@@ -406,7 +443,7 @@
         b_proj,
         c_proj,
         state_pool,
-        conv_pool,
+        conv_pool.transpose(1, 0, 2),
         conv_weight,
         conv_bias[None],
         step_bias[None],
@@ -435,7 +472,7 @@
             sem(()),
             weights,
             weights,
-            weights,
+            pltpu.VMEM((units, d), BF16),
             sem((3, nch)),
             pltpu.VMEM((rows_dev, chl + LANES), BF16),
             pltpu.VMEM((peers, rows_dev, chl + LANES), BF16),
@@ -453,8 +490,9 @@
             sem((peers,)),
             sem((peers,)),
             pltpu.VMEM((rows, d), F32),
-            pltpu.VMEM((rows, d), BF16),
-            pltpu.VMEM((nch, 2 * rows, ub), BF16),
+            pltpu.VMEM((nch, rows, ub), F32),
+            pltpu.VMEM((nch, rows, ub), F32),
+            pltpu.VMEM((2 * rows, units), BF16),
             pltpu.VMEM((NJ, peers, rows_dev, cw), BF16),
             pltpu.VMEM((NJ // 2, 2 * peers, rows_dev, cw), BF16),
             sem((NJ, peers)),

time: 49.8 us -> 43.5 us (0.87)
  Pallas kernels: 44.4 us -> 39.5 us
  local copies, waits for them, and re-layouts: 4.48 us -> 3 us
    pallas_call x1, Pallas kernels: 44.4 us -> 39.5 us  [local(): pl.pallas_call(functools.partial(kernel, peers), out_shape=(jax.ShapeDtyp...]
    unnamed x3 -> x2, local copies, waits for them, and re-layouts: 4.48 us -> 3 us
where the time goes in v2:
time: 43.5 us; the launch traced here: 43.2 us
  Pallas kernels  39.5 us (91%)
  local copies, waits for them, and re-layouts  3 us (7%)
  between operations  0.65 us (1%)
    pallas_call x1, Pallas kernels, local(): pl.pallas_call(functools.partial(kernel, peers), out_shape=(jax.ShapeDtyp...  39.5 us
    unnamed x2, local copies, waits for them, and re-layouts  3 us

profile of v2, /device:TPU:0, one launch (start us, length us, event | category | flops | bytes accessed | tf_op | source)
XLA Modules:
  0.0 43.2 jit_solution(14727331572004605686)
XLA Ops:
  0.6 39.5 %shard_map.212 = (bf16[2,4096]{1,0:T(2,128)(2,1)}, bf16[2,16,4096]{2,1,0:T(8,128)(2,1)}) custom-call(s32[2]{0:T(128)} %slots.1, bf16[2,4096]{1,0:T(2,128)(2,1)} %refs_0_.1, bf16[2,4096]{1,0:T(2,128)(2,1)} %refs_1_.1, bf16[2,4096]{1,0:T(2,128)(2,1)} %refs_2_.1, f32[2,16]{1,0:T(2,128)} %refs_3_.1, f32[2,16]{1,0:T(2,128)} %refs_4_.1, ...), custom_call_target="tpu_custom_call" | custom-call | tf_op jit(solution)/shard_map/pallas_call | solution.py:460
  40.2 1.3 %copy.25 = bf16[2,4096]{1,0:T(2,128)(2,1)} copy(bf16[2,4096]{1,0:T(2,128)(2,1)} %get-tuple-element.4) | data formatting | bytes 32768
  41.5 1.7 %copy.26 = bf16[2,16,4096]{2,1,0:T(8,128)(2,1)} copy(bf16[2,16,4096]{2,1,0:T(8,128)(2,1)} %get-tuple-element.5) | data formatting | bytes 524288
